TPU v7x, 512 devices: a whole 4x4x16 slice. The times are simulated.
512 devices in a mesh: rowg: 16 (over y_hi, x, core), colg: 32 (over y_lo, z).
Axes of the slice: x: 4, y: 4 (y_hi: 2, y_lo: 2; y = y_hi * 2 + y_lo), z: 16, core: 2. Of those that a mesh axis runs over, the one named last changes fastest.
Arguments:
- pair_rows: int32 [8192, 32768], P('rowg', 'colg'), may hold values from 0 to 240
- reducers: int32 [2, 1024, 32768], P(None, 'rowg', 'colg'), may hold values from 0 to 240
- pivots: int32 [2, 1024], replicated, may hold values from 0 to 32767, as said below
- counts: int32 [16], replicated, may hold values from 0 to 512, as said below
Outputs:
- reduced: int32 [4096, 32768], P('rowg', 'colg')
Inputs may be any that keep to these rules, and one draw needn't show every extreme that they name: `pivots`: the 2048 pivot columns are all different; column 0 and column 32767 are among them. `counts`: owners 2i and 2i + 1 together hold 512 live rows; some owner has exactly 512 live rows and its partner none; owner 16 - 2 holds more than 256 live rows.
All inputs are finite; a program needn't handle non-finite values.
Results may differ from a plain program's by a relative error of at most 0.000001.
Values may be sent and summed in bfloat16 or wider, within the bound.
No kernel may reach another device: no remote copies, remote signals or barrier semaphores. Data moves between devices by JAX's collectives and lax.ppermute only.
A program may use at most 64 MiB of HBM per device.

v0:
```python
import jax
import jax.numpy as jnp
from jax import lax
from jax.sharding import PartitionSpec as P

PANELS = 2
LIVE_DEV = 256
modulus = 241.0
half_modulus = 120.0


def partner_2(value, axis, stride):
    return lax.ppermute(value, axis, [(i, i ^ 1 << stride) for i in range(lax.axis_size(axis))])


def centered(values):
    return values - modulus * (values > half_modulus).astype(values.dtype)


def pick_value(table, position):
    marks = lax.iota(jnp.int32, table.shape[0]) == position
    return jnp.sum(jnp.where(marks, table, jnp.zeros_like(table)))


def place_rows(source, my_start, my_count, target, live_dev):
    slot_count = source.shape[0]
    rank_ids = target * live_dev + lax.iota(jnp.int32, live_dev)
    offsets = rank_ids - my_start
    valid = (offsets >= 0) & (offsets < my_count)
    picked = jnp.take(source, jnp.clip(offsets, 0, slot_count - 1), axis=0)
    return jnp.where(valid[:, None], picked, jnp.zeros_like(picked))


def normalize_block(block, pivot_cols, all_pivots, row_index, col_start):
    block_rows = block.shape[0]
    col_width = block.shape[1]
    columns = col_start + lax.iota(jnp.int32, col_width)
    is_pivot = jnp.any(columns[:, None] == all_pivots[None, :], axis=1)
    own_cols = lax.dynamic_slice_in_dim(pivot_cols, row_index * block_rows, block_rows)
    own_pivot = columns[None, :] == own_cols[:, None]
    entries = centered(block.astype(jnp.float32))
    ones = jnp.ones_like(entries)
    zeros = jnp.zeros_like(entries)
    kept = jnp.where(is_pivot[None, :], jnp.where(own_pivot, ones, zeros), entries)
    return kept.astype(jnp.bfloat16)


def local_columns(matrix_rows, pivot_cols, col_start):
    col_width = matrix_rows.shape[1]
    offsets = pivot_cols - col_start
    inside = (offsets >= 0) & (offsets < col_width)
    taken = jnp.take(matrix_rows, jnp.clip(offsets, 0, col_width - 1), axis=1)
    return jnp.where(inside[None, :], taken, jnp.zeros_like(taken)).astype(jnp.bfloat16)


def folded_product(factors, normed):
    return jnp.dot(
        factors,
        lax.all_gather(normed, "rowg", axis=0, tiled=True),
        preferred_element_type=jnp.float32,
    )


def shards(pair_rows, reducers, pivots, counts):
    row_index = lax.axis_index("rowg")
    col_index = lax.axis_index("colg")
    col_width = pair_rows.shape[1]
    col_start = col_index * col_width
    live_dev = LIVE_DEV
    partner = row_index + 1 - 2 * (row_index % 2)
    ends = jnp.cumsum(counts)
    starts = ends - counts
    my_start = pick_value(starts, row_index)
    my_count = pick_value(counts, row_index)
    all_pivots = pivots.reshape(-1)
    normed_list = [
        normalize_block(reducers[panel], pivots[panel], all_pivots, row_index, col_start)
        for panel in range(PANELS)
    ]
    matrix_rows = pair_rows.astype(jnp.float32)
    for panel in range(PANELS):
        taken = local_columns(matrix_rows, pivots[panel], col_start)
        summed = lax.psum(taken, "colg").astype(jnp.float32)
        factors = centered(summed).astype(jnp.bfloat16)
        product = folded_product(factors, normed_list[panel])
        matrix_rows = jnp.mod(matrix_rows - product, modulus)
    source = matrix_rows.astype(jnp.bfloat16)
    kept = place_rows(source, my_start, my_count, row_index, live_dev)
    outgoing = place_rows(source, my_start, my_count, partner, live_dev)
    incoming = partner_2(outgoing, "rowg", 0)
    result = kept.astype(jnp.float32) + incoming.astype(jnp.float32)
    return result.astype(jnp.int32)


def solution(mesh):
    return jax.shard_map(
        shards,
        mesh=mesh,
        in_specs=(P("rowg", "colg"), P(None, "rowg", "colg"), P(), P()),
        out_specs=P("rowg", "colg"),
        check_vma=False,
    )
```

profile of v0, /device:TPU:1, one launch (start us, length us, event | category | flops | bytes accessed | tf_op | source)
XLA Modules:
  0.0 569.9 jit_solution(17326288771651892807)
XLA Ops:
  7.4 0.8 subtract_clamp_fusion
  8.2 0.8 and_reduce_fusion
  9.0 1.8 convert_element_type.55
  10.9 0.5 copy.16
  11.4 4.0 gather_fusion
  15.9 1.2 fusion.4
  17.4 1.2 compare_reduce_fusion
  18.5 1.9 fusion.14
  21.1 240.5 %all-reduce.3.cloned.1.call-done = bf16[512,1024]{1,0:T(8,128)(2,1)} async-done(((bf16[512,1024]{1,0:T(8,128)(2,1)}), bf16[512,1024]{1,0:T(8,128)(2,1)}) %all-reduce.3.cloned.1.call-update) | async-done | bytes 1048592 | tf_op jit(solution)/shard_map/psum | solution.py:83
  261.6 5.4 add_select_fusion.1
  267.0 1.8 copy.18
  268.8 4.0 gather_fusion.1
  273.3 1.2 fusion.3
  274.8 0.7 fusion.20
  275.5 0.6 compare_select_fusion.2
  276.2 1.3 compare_and_fusion.2
  277.5 250.6 %all-reduce.5.cloned.1.call-done = bf16[512,1024]{1,0:T(8,128)(2,1)} async-done(((bf16[512,1024]{1,0:T(8,128)(2,1)}), bf16[512,1024]{1,0:T(8,128)(2,1)}) %all-reduce.5.cloned.1.call-update) | async-done | bytes 1048592 | tf_op jit(solution)/shard_map/psum | solution.py:83
  528.1 4.1 fusion.2
  532.2 1.2 gather_fusion.3
  533.5 24.6 %collective-permute-start = (bf16[256,1024]{1,0:T(8,128)(2,1)S(1)}, bf16[256,1024]{1,0:T(8,128)(2,1)S(1)}, u32[]{:S(2)}, u32[]{:S(2)}) collective-permute-start(bf16[256,1024]{1,0:T(8,128)(2,1)S(1)} %select_select_fusion), channel_id=1, source_target_pairs={{0,32},{32,0},{64,96},{96,64},{128,160},{160,128},{192,224},{224,1... | collective-permute-start | bytes 1572872 | tf_op jit(solution)/shard_map/ppermute | solution.py:13
  558.1 0.6 compare_select_fusion.3
  558.7 1.3 compare_and_fusion.3
  560.0 1.2 gather_fusion.2
  561.2 1.3 add_convert_fusion
  (34 shorter events, 2.3 us)
Async XLA Ops:
  7.4 254.2 %all-reduce.3.cloned.1.call-start = ((), (), s32[]{:S(2)}) async-start(), calls=%async_computation | async-start | bytes 2097152 | tf_op jit(solution)/shard_map/psum | solution.py:83
  15.9 1.3 copy-start.2
  15.9 245.7 %copy-start = (s32[512,1024]{1,0:T(8,128)S(1)}, s32[512,1024]{1,0:T(8,128)}, u32[]{:S(2)}) copy-start(s32[512,1024]{1,0:T(8,128)} %param.8) | copy-start | bytes 6291460
  17.2 244.4 %all-gather.3.cloned.1.call-start = ((), (), s32[]{:S(2)}) async-start(), calls=%async_computation.1 | async-start | bytes 2228224 | tf_op jit(solution)/shard_map/all_gather | solution.py:59
  20.4 257.1 %all-gather.5.cloned.1.call-start = ((), (), s32[]{:S(2)}) async-start(), calls=%async_computation.3 | async-start | bytes 2228224 | tf_op jit(solution)/shard_map/all_gather | solution.py:59
  21.0 507.1 %all-reduce.5.cloned.1.call-start = ((), (), s32[]{:S(2)}) async-start(), calls=%async_computation.2 | async-start | bytes 2097152 | tf_op jit(solution)/shard_map/psum | solution.py:83
  273.3 1.3 copy-start.3
  273.3 254.8 %copy-start.1 = (f32[512,1024]{1,0:T(8,128)S(1)}, f32[512,1024]{1,0:T(8,128)}, u32[]{:S(2)}) copy-start(f32[512,1024]{1,0:T(8,128)} %add_select_fusion.1) | copy-start | bytes 6291460
  533.5 27.7 %collective-permute-start = (bf16[256,1024]{1,0:T(8,128)(2,1)S(1)}, bf16[256,1024]{1,0:T(8,128)(2,1)S(1)}, u32[]{:S(2)}, u32[]{:S(2)}) collective-permute-start(bf16[256,1024]{1,0:T(8,128)(2,1)S(1)} %select_select_fusion), channel_id=1, source_target_pairs={{0,32},{32,0},{64,96},{96,64},{128,160},{160,128},{192,224},{224,1... | collective-permute-start | bytes 1572872 | tf_op jit(solution)/shard_map/ppermute | solution.py:13
Sparse Core Ops, SparseCore 0:
  17.3 244.2 all-reduce.2
  274.7 253.3 all-reduce.4
Sparse Core Ops, SparseCore 1:
  21.0 69.8 all-gather.2
  94.1 62.1 all-gather.4
where the time goes:
time: 570 us
  waiting for transfers between devices  492 us (86%)
  starting transfers between devices  24.7 us (4%)
  other arithmetic  15.1 us (3%)
  between operations  15.1 us (3%)
  local copies, waits for them, and re-layouts  13.8 us (2%)
  matrix products  9.46 us (2%)
    psum x2, waiting for transfers between devices, shards(): summed = lax.psum(taken, 'colg').astype(jnp.float32)  491 us
    ppermute x1, starting transfers between devices, partner_2(): lax.ppermute(value, axis, [(i, i ^ 1 << stride) for i in range(lax.axis_s...  24.6 us
  transfers between devices with their start and end apart: 5, of which 2 were waited for; matrix products, arithmetic and copies ran while one was open for 4% of the time, Pallas kernels for 0%

commit v1 on v0

--- a/solution.py
+++ b/solution.py
@@ -80,7 +80,7 @@
     matrix_rows = pair_rows.astype(jnp.float32)
     for panel in range(PANELS):
         taken = local_columns(matrix_rows, pivots[panel], col_start)
-        summed = lax.psum(taken, "colg").astype(jnp.float32)
+        summed = jnp.sum(lax.all_gather(taken, "colg"), axis=0).astype(jnp.float32)
         factors = centered(summed).astype(jnp.bfloat16)
         product = folded_product(factors, normed_list[panel])
         matrix_rows = jnp.mod(matrix_rows - product, modulus)

time: 570 us -> 924 us (1.62)
  waiting for transfers between devices: 492 us -> 846 us
  other arithmetic: 15.1 us -> 38.4 us
  starting transfers between devices: 24.7 us -> 2.33 us
    all_gather x0 -> x2, waiting for transfers between devices: none -> 741 us  [shards(): summed = jnp.sum(lax.all_gather(taken, 'colg'), axis=0).astype(jnp.float32)]
    psum x2 -> x0, waiting for transfers between devices: 491 us -> none  [shards(): summed = lax.psum(taken, 'colg').astype(jnp.float32)]
    all_gather x2, waiting for transfers between devices: 0.03 us -> 105 us  [folded_product(): lax.all_gather(normed, 'rowg', axis=0, tiled=True)]
    reduce_sum x0 -> x2, other arithmetic: none -> 24.2 us  [shards(): summed = jnp.sum(lax.all_gather(taken, 'colg'), axis=0).astype(jnp.float32)]
    ppermute x1, starting transfers between devices: 24.6 us -> 2.2 us  [partner_2(): lax.ppermute(value, axis, [(i, i ^ 1 << stride) for i in range(lax.axis_s...]
  transfers between devices with their start and end apart: 5 -> 5, of which waited for: 2 -> 4; matrix products, arithmetic and copies ran while one was open for 4% -> 4% of each run, Pallas kernels for 0% -> 0%
where the time goes in v1:
time: 924 us; the launch traced here: 923 us
  waiting for transfers between devices  846 us (92%)
  other arithmetic  38.4 us (4%)
  local copies, waits for them, and re-layouts  13.8 us (1%)
  between operations  13.4 us (1%)
    all_gather x2, waiting for transfers between devices, shards(): summed = jnp.sum(lax.all_gather(taken, 'colg'), axis=0).astype(jnp.float32)  741 us
    all_gather x2, waiting for transfers between devices, folded_product(): lax.all_gather(normed, 'rowg', axis=0, tiled=True)  105 us
    reduce_sum x2, other arithmetic, shards(): summed = jnp.sum(lax.all_gather(taken, 'colg'), axis=0).astype(jnp.float32)  24.2 us
  transfers between devices with their start and end apart: 5, of which 4 were waited for; matrix products, arithmetic and copies ran while one was open for 4% of the time, Pallas kernels for 0%

profile of v1, /device:TPU:1, one launch (start us, length us, event | category | flops | bytes accessed | tf_op | source)
XLA Modules:
  0.0 923.3 jit_solution(17085766376963555098)
XLA Ops:
  6.5 0.8 subtract_clamp_fusion
  7.4 0.8 and_reduce_fusion
  8.2 1.8 convert_element_type.59
  10.6 4.0 gather_fusion
  15.1 1.2 fusion.4
  16.5 1.2 compare_reduce_fusion
  17.7 0.8 fusion.14
  18.6 374.5 %all-gather.11.cloned.1.call-done = bf16[16384,1024]{1,0:T(8,128)(2,1)} async-done(((bf16[512,1024]{1,0:T(8,128)(2,1)}), bf16[16384,1024]{1,0:T(8,128)(2,1)}) %all-gather.11.cloned.1.call-update) | async-done | bytes 33554448 | tf_op jit(solution)/shard_map/all_gather | solution.py:83
  393.1 11.6 %reduce_sum.44 = bf16[512,1024]{1,0:T(8,128)(2,1)S(1)} reduce(bf16[32,512,1024]{2,1,0:T(8,128)(2,1)} %bitcast.42, bf16[]{:T(256)} %constant.52.clone.1), dimensions={0}, to_apply=%region_3.5 | reduce | flops 16252928 | bytes 34603008 | tf_op jit(solution)/shard_map/reduce_sum | solution.py:83
  404.8 52.9 %all-gather.7.cloned.1.call-done = bf16[1024,1024]{1,0:T(8,128)(2,1)} async-done(((bf16[64,1024]{1,0:T(8,128)(2,1)}), bf16[1024,1024]{1,0:T(8,128)(2,1)}) %all-gather.7.cloned.1.call-update) | async-done | bytes 2097168 | tf_op jit(solution)/shard_map/all_gather | solution.py:59
  457.6 5.0 add_select_fusion.1
  462.6 1.8 copy.18
  464.4 4.0 gather_fusion.1
  468.9 1.2 fusion.3
  472.4 1.3 compare_and_fusion.2
  473.8 366.6 %all-gather.13.cloned.1.call-done = bf16[16384,1024]{1,0:T(8,128)(2,1)} async-done(((bf16[512,1024]{1,0:T(8,128)(2,1)}), bf16[16384,1024]{1,0:T(8,128)(2,1)}) %all-gather.13.cloned.1.call-update) | async-done | bytes 33554448 | tf_op jit(solution)/shard_map/all_gather | solution.py:83
  840.3 12.6 %reduce_sum.45 = bf16[512,1024]{1,0:T(8,128)(2,1)} reduce(bf16[32,512,1024]{2,1,0:T(8,128)(2,1)} %bitcast.41, bf16[]{:T(256)} %constant.52.clone.1), dimensions={0}, to_apply=%region_5.7 | reduce | flops 16252928 | bytes 34603008 | tf_op jit(solution)/shard_map/reduce_sum | solution.py:83
  852.9 51.8 %all-gather.9.cloned.1.call-done = bf16[1024,1024]{1,0:T(8,128)(2,1)} async-done(((bf16[64,1024]{1,0:T(8,128)(2,1)}), bf16[1024,1024]{1,0:T(8,128)(2,1)}) %all-gather.9.cloned.1.call-update) | async-done | bytes 2097168 | tf_op jit(solution)/shard_map/all_gather | solution.py:59
  904.7 4.1 fusion.2
  908.7 1.2 gather_fusion.3
  910.1 2.2 collective-permute-start
  913.0 1.3 compare_and_fusion.3
  914.3 1.2 gather_fusion.2
  915.5 1.3 add_convert_fusion
  (38 shorter events, 4.9 us)
Async XLA Ops:
  6.5 386.6 %all-gather.11.cloned.1.call-start = ((), (), s32[]{:S(2)}) async-start(), calls=%async_computation.2 | async-start | bytes 34603008 | tf_op jit(solution)/shard_map/all_gather | solution.py:83
  15.1 1.3 copy-start.3
  15.1 2.6 copy-start.2
  16.4 441.2 %all-gather.7.cloned.1.call-start = ((), (), s32[]{:S(2)}) async-start(), calls=%async_computation | async-start | bytes 2228224 | tf_op jit(solution)/shard_map/all_gather | solution.py:59
  18.6 821.8 %all-gather.13.cloned.1.call-start = ((), (), s32[]{:S(2)}) async-start(), calls=%async_computation.3 | async-start | bytes 34603008 | tf_op jit(solution)/shard_map/all_gather | solution.py:83
  393.1 64.5 %copy-start = (s32[512,1024]{1,0:T(8,128)S(1)}, s32[512,1024]{1,0:T(8,128)}, u32[]{:S(2)}) copy-start(s32[512,1024]{1,0:T(8,128)} %param.8) | copy-start | bytes 6291460
  468.9 1.9 copy-start.4
  470.2 434.5 %all-gather.9.cloned.1.call-start = ((), (), s32[]{:S(2)}) async-start(), calls=%async_computation.1 | async-start | bytes 2228224 | tf_op jit(solution)/shard_map/all_gather | solution.py:59
  840.3 64.3 %copy-start.1 = (f32[512,1024]{1,0:T(8,128)S(1)}, f32[512,1024]{1,0:T(8,128)}, u32[]{:S(2)}) copy-start(f32[512,1024]{1,0:T(8,128)} %add_select_fusion.1) | copy-start | bytes 6291460
  910.1 5.4 collective-permute-start
Sparse Core Ops, SparseCore 0:
  16.5 376.6 all-gather.10
  396.5 61.1 all-gather.6
  470.3 369.9 all-gather.12
  843.5 61.1 all-gather.8
